TPU v7x, 32 devices: a whole 2x2x4 slice. The times are simulated.
32 devices in a mesh: grp: 2 (over x), blk: 16 (over z, y, core).
Axes of the slice: x: 2, y: 2, z: 4, core: 2. Of those that a mesh axis runs over, the one named last changes fastest.
Arguments:
- e_field: float32 [3, 128, 64, 128], P(None, 'blk', 'grp'), may hold values from -6 to 6
- h_field: float32 [3, 128, 64, 128], P(None, 'blk', 'grp'), may hold values from -6 to 6
- inv_eps: float32 [128, 64, 128], P('blk', 'grp'), may hold values from 0.08 to 1
- cot_e: float32 [3, 128, 64, 128], P(None, 'blk', 'grp'), may hold values from -6 to 6
- cot_h: float32 [3, 128, 64, 128], P(None, 'blk', 'grp'), may hold values from -6 to 6
- voxel_ids: int32 [128, 64, 128], P('blk', 'grp'), may hold values from 0 to 2047
Outputs:
- e_final: float32 [3, 128, 64, 128], P(None, 'blk', 'grp')
- h_final: float32 [3, 128, 64, 128], P(None, 'blk', 'grp')
- voxel_grad: float32 [2048], P(('grp', 'blk'))
All inputs are finite; a program needn't handle non-finite values.
Results may differ from a plain program's by a relative error of at most 0.0001.
Values sent between devices are 32-bit elements; how exact they have to be, the bound alone decides.
A program may use at most 64 MiB of HBM per device.

v0:
```python
import jax
import jax.numpy as jnp
from jax import lax
from jax.sharding import PartitionSpec as P

VOX_DEV = 64
STEPS = 4


courant = 0.5


def passed_along(value, axis, steps):
    count = lax.axis_size(axis)
    first, last = (max(0, -steps), min(count, count - steps))
    return lax.ppermute(value, axis, [(source, source + steps) for source in range(first, last)])


def curl_forward(field):
    upper_xf = passed_along(field[1:3, :1], "blk", -1)
    upper_zf = passed_along(field[0:2, :, :1], "grp", -1)
    dx_yz = jnp.concatenate([field[1:3, 1:], upper_xf], axis=1) - field[1:3]
    dz_xy = jnp.concatenate([field[0:2, :, 1:], upper_zf], axis=2) - field[0:2]
    pair_xz = jnp.stack([field[0], field[2]])
    dy_xz = (
        jnp.concatenate([pair_xz[:, :, :, 1:], jnp.zeros_like(pair_xz[:, :, :, :1])], axis=3)
        - pair_xz
    )
    curl_x = dy_xz[1] - dz_xy[1]
    curl_y = dz_xy[0] - dx_yz[1]
    curl_z = dx_yz[0] - dy_xz[0]
    return jnp.stack([curl_x, curl_y, curl_z])


def curl_backward(field):
    lower_xf = passed_along(field[1:3, -1:], "blk", 1)
    lower_zf = passed_along(field[0:2, :, -1:], "grp", 1)
    dx_yz = field[1:3] - jnp.concatenate([lower_xf, field[1:3, :-1]], axis=1)
    dz_xy = field[0:2] - jnp.concatenate([lower_zf, field[0:2, :, :-1]], axis=2)
    pair_xz = jnp.stack([field[0], field[2]])
    dy_xz = pair_xz - jnp.concatenate(
        [jnp.zeros_like(pair_xz[:, :, :, :1]), pair_xz[:, :, :, :-1]], axis=3
    )
    curl_x = dy_xz[1] - dz_xy[1]
    curl_y = dz_xy[0] - dx_yz[1]
    curl_z = dx_yz[0] - dy_xz[0]
    return jnp.stack([curl_x, curl_y, curl_z])


def local(e_field, h_field, inv_eps, cot_e, cot_h, voxel_ids):
    curls = []
    for step in range(STEPS):
        h_field = h_field - courant * curl_forward(e_field)
        curl_now = curl_backward(h_field)
        curls.append(curl_now)
        e_field = e_field + courant * inv_eps[None] * curl_now
    adj_e, adj_h = (cot_e, cot_h)
    grad = jnp.zeros(inv_eps.shape, jnp.float32)
    for step in range(STEPS - 1, -1, -1):
        adj_h = adj_h + courant * curl_forward(inv_eps[None] * adj_e)
        grad = grad + courant * jnp.sum(adj_e * curls[step], axis=0)
        adj_e = adj_e - courant * curl_backward(adj_h)
    total_vox = VOX_DEV * lax.axis_size("grp") * lax.axis_size("blk")
    partial_vec = jax.ops.segment_sum(
        grad.reshape(-1), voxel_ids.reshape(-1), num_segments=total_vox
    )
    voxel_grad = lax.psum_scatter(partial_vec, ("grp", "blk"), scatter_dimension=0, tiled=True)
    return (e_field, h_field, voxel_grad)


def solution(mesh):
    placed = (
        P(None, "blk", "grp", None),
        P(None, "blk", "grp", None),
        P("blk", "grp", None),
        P(None, "blk", "grp", None),
        P(None, "blk", "grp", None),
        P("blk", "grp", None),
    )
    return jax.shard_map(
        local,
        mesh=mesh,
        in_specs=placed,
        out_specs=(P(None, "blk", "grp", None), P(None, "blk", "grp", None), P(("grp", "blk"))),
        check_vma=False,
    )
```

profile of v0, /device:TPU:0, one launch (start us, length us, event | category | flops | bytes accessed | tf_op | source)
XLA Modules:
  0.0 325.7 jit_solution(17179817309714988779)
XLA Ops:
  0.6 1.1 broadcast_multiply_fusion.2
  1.8 1.3 collective-permute-start.16
  3.1 1.3 collective-permute-start.17
  4.4 1.3 collective-permute-start
  5.7 1.3 collective-permute-start.1
  7.1 0.9 copy-done.4
  8.7 0.9 copy-done.3
  10.4 0.9 copy-done.2
  11.5 4.3 %collective-permute-start.18 = (f32[2,8,1,128]{3,2,1,0:T(1,128)S(1)}, f32[2,8,1,128]{3,2,1,0:T(1,128)S(1)}, u32[]{:S(2)}, u32[]{:S(2)}) collective-permute-start(f32[2,8,1,128]{3,2,1,0:T(1,128)S(1)} %slice.982), channel_id=1, source_target_pairs={{0,16},{1,17},{2,18},{3,19},{4,20},{5,21},{6,22},{7,23},{8,24},{9,... | collective-permute-start | bytes 24584 | tf_op jit(solution)/shard_map/ppermute | solution.py:16
  15.8 4.5 %collective-permute-start.19 = (f32[2,1,32,128]{3,2,1,0:T(8,128)S(1)}, f32[2,1,32,128]{3,2,1,0:T(8,128)S(1)}, u32[]{:S(2)}, u32[]{:S(2)}) collective-permute-start(f32[2,1,32,128]{3,2,1,0:T(8,128)S(1)} %slice.987), channel_id=1, source_target_pairs={{0,1},{1,2},{2,3},{3,4},{4,5},{5,6},{6,7},{7,8},{8,9},{9,10},{10,1... | collective-permute-start | bytes 98312 | tf_op jit(solution)/shard_map/ppermute | solution.py:16
  20.5 1.6 collective-permute-start.2
  22.1 3.1 collective-permute-start.3
  25.4 0.6 collective-permute-done.3
  26.3 1.3 collective-permute-start.4
  27.6 1.3 collective-permute-start.5
  29.3 2.6 collective-permute-done.4
  32.7 4.3 %collective-permute-start.6 = (f32[2,8,1,128]{3,2,1,0:T(1,128)S(1)}, f32[2,8,1,128]{3,2,1,0:T(1,128)S(1)}, u32[]{:S(2)}, u32[]{:S(2)}) collective-permute-start(f32[2,8,1,128]{3,2,1,0:T(1,128)S(1)} %slice.886), channel_id=1, source_target_pairs={{0,16},{1,17},{2,18},{3,19},{4,20},{5,21},{6,22},{7,23},{8,24},{9,... | collective-permute-start | bytes 24584 | tf_op jit(solution)/shard_map/ppermute | solution.py:16
  37.0 5.1 %collective-permute-start.7 = (f32[2,1,32,128]{3,2,1,0:T(8,128)S(1)}, f32[2,1,32,128]{3,2,1,0:T(8,128)S(1)}, u32[]{:S(2)}, u32[]{:S(2)}) collective-permute-start(f32[2,1,32,128]{3,2,1,0:T(8,128)S(1)} %slice.891), channel_id=1, source_target_pairs={{0,1},{1,2},{2,3},{3,4},{4,5},{5,6},{6,7},{7,8},{8,9},{9,10},{10,1... | collective-permute-start | bytes 98312 | tf_op jit(solution)/shard_map/ppermute | solution.py:16
  42.3 0.6 collective-permute-done.7
  43.3 1.3 collective-permute-start.8
  44.6 1.3 collective-permute-start.9
  46.1 2.7 collective-permute-done.8
  49.2 3.4 %collective-permute-start.10 = (f32[2,8,1,128]{3,2,1,0:T(1,128)S(1)}, f32[2,8,1,128]{3,2,1,0:T(1,128)S(1)}, u32[]{:S(2)}, u32[]{:S(2)}) collective-permute-start(f32[2,8,1,128]{3,2,1,0:T(1,128)S(1)} %slice.918), channel_id=1, source_target_pairs={{0,16},{1,17},{2,18},{3,19},{4,20},{5,21},{6,22},{7,23},{8,24},{9,... | collective-permute-start | bytes 24584 | tf_op jit(solution)/shard_map/ppermute | solution.py:16
  52.7 4.8 %collective-permute-start.11 = (f32[2,1,32,128]{3,2,1,0:T(8,128)S(1)}, f32[2,1,32,128]{3,2,1,0:T(8,128)S(1)}, u32[]{:S(2)}, u32[]{:S(2)}) collective-permute-start(f32[2,1,32,128]{3,2,1,0:T(8,128)S(1)} %slice.923), channel_id=1, source_target_pairs={{0,1},{1,2},{2,3},{3,4},{4,5},{5,6},{6,7},{7,8},{8,9},{9,10},{10,1... | collective-permute-start | bytes 98312 | tf_op jit(solution)/shard_map/ppermute | solution.py:16
  57.7 0.6 collective-permute-done.11
  58.7 1.3 collective-permute-start.12
  60.0 1.3 collective-permute-start.13
  61.5 2.7 collective-permute-done.12
  64.7 3.4 %collective-permute-start.14 = (f32[2,8,1,128]{3,2,1,0:T(1,128)S(1)}, f32[2,8,1,128]{3,2,1,0:T(1,128)S(1)}, u32[]{:S(2)}, u32[]{:S(2)}) collective-permute-start(f32[2,8,1,128]{3,2,1,0:T(1,128)S(1)} %slice.950), channel_id=1, source_target_pairs={{0,16},{1,17},{2,18},{3,19},{4,20},{5,21},{6,22},{7,23},{8,24},{9,... | collective-permute-start | bytes 24584 | tf_op jit(solution)/shard_map/ppermute | solution.py:16
  68.1 5.0 %collective-permute-start.15 = (f32[2,1,32,128]{3,2,1,0:T(8,128)S(1)}, f32[2,1,32,128]{3,2,1,0:T(8,128)S(1)}, u32[]{:S(2)}, u32[]{:S(2)}) collective-permute-start(f32[2,1,32,128]{3,2,1,0:T(8,128)S(1)} %slice.955), channel_id=1, source_target_pairs={{0,1},{1,2},{2,3},{3,4},{4,5},{5,6},{6,7},{7,8},{8,9},{9,10},{10,1... | collective-permute-start | bytes 98312 | tf_op jit(solution)/shard_map/ppermute | solution.py:16
  73.3 0.6 collective-permute-done.15
  74.2 0.8 copy-done.5
  75.0 1.1 multiply_reduce_fusion.2
  76.2 1.3 collective-permute-start.20
  77.5 1.3 collective-permute-start.21
  79.1 2.7 collective-permute-done.20
  82.1 3.4 %collective-permute-start.22 = (f32[2,8,1,128]{3,2,1,0:T(1,128)S(1)}, f32[2,8,1,128]{3,2,1,0:T(1,128)S(1)}, u32[]{:S(2)}, u32[]{:S(2)}) collective-permute-start(f32[2,8,1,128]{3,2,1,0:T(1,128)S(1)} %slice.1014), channel_id=1, source_target_pairs={{0,16},{1,17},{2,18},{3,19},{4,20},{5,21},{6,22},{7,23},{8,24},{9,... | collective-permute-start | bytes 24584 | tf_op jit(solution)/shard_map/ppermute | solution.py:16
  85.5 5.7 %collective-permute-start.23 = (f32[2,1,32,128]{3,2,1,0:T(8,128)S(1)}, f32[2,1,32,128]{3,2,1,0:T(8,128)S(1)}, u32[]{:S(2)}, u32[]{:S(2)}) collective-permute-start(f32[2,1,32,128]{3,2,1,0:T(8,128)S(1)} %slice.1019), channel_id=1, source_target_pairs={{0,1},{1,2},{2,3},{3,4},{4,5},{5,6},{6,7},{7,8},{8,9},{9,10},{10,1... | collective-permute-start | bytes 98312 | tf_op jit(solution)/shard_map/ppermute | solution.py:16
  91.4 0.6 collective-permute-done.23
  92.4 1.3 collective-permute-start.24
  93.7 1.3 collective-permute-start.25
  95.2 2.7 collective-permute-done.24
  98.3 3.4 %collective-permute-start.26 = (f32[2,8,1,128]{3,2,1,0:T(1,128)S(1)}, f32[2,8,1,128]{3,2,1,0:T(1,128)S(1)}, u32[]{:S(2)}, u32[]{:S(2)}) collective-permute-start(f32[2,8,1,128]{3,2,1,0:T(1,128)S(1)} %slice.1046), channel_id=1, source_target_pairs={{0,16},{1,17},{2,18},{3,19},{4,20},{5,21},{6,22},{7,23},{8,24},{9,... | collective-permute-start | bytes 24584 | tf_op jit(solution)/shard_map/ppermute | solution.py:16
  101.7 5.7 %collective-permute-start.27 = (f32[2,1,32,128]{3,2,1,0:T(8,128)S(1)}, f32[2,1,32,128]{3,2,1,0:T(8,128)S(1)}, u32[]{:S(2)}, u32[]{:S(2)}) collective-permute-start(f32[2,1,32,128]{3,2,1,0:T(8,128)S(1)} %slice.1051), channel_id=1, source_target_pairs={{0,1},{1,2},{2,3},{3,4},{4,5},{5,6},{6,7},{7,8},{8,9},{9,10},{10,1... | collective-permute-start | bytes 98312 | tf_op jit(solution)/shard_map/ppermute | solution.py:16
  107.6 0.6 collective-permute-done.27
  108.8 172.7 %scatter_custom_fusion = f32[2048]{0:T(1024)S(1)} fusion(s32[32768]{0:T(1024)} %bitcast.3, f32[32768]{0:T(1024)S(1)} %bitcast.2, f32[]{:T(128)} %constant.3.clone.1), kind=kCustom, calls=%fused_computation.179 | custom fusion | flops 32768 | bytes 8704 | tf_op jit(solution)/shard_map/scatter-add | solution.py:64
  281.5 43.7 %all-reduce.14 = f32[2048]{0:T(1024)S(1)} all-reduce(f32[2048]{0:T(1024)S(1)} %scatter_custom_fusion), channel_id=2, replica_groups=mesh['grp'=2,'blk'=16] {'grp','blk'}, use_global_device_ids=true, to_apply=%region_5.0.clone | all-reduce | flops 2048 | bytes 16384
  325.1 0.6 dynamic-slice
  (164 shorter events, 8.3 us)
Async XLA Ops:
  0.6 3.8 %copy-start = (f32[3,8,32,128]{3,2,1,0:T(8,128)S(1)}, f32[3,8,32,128]{3,2,1,0:T(8,128)}, u32[]{:S(2)}) copy-start(f32[3,8,32,128]{3,2,1,0:T(8,128)} %param.6) | copy-start | bytes 1179652
  1.8 6.7 %collective-permute-start.16 = (f32[2,8,1,128]{3,2,1,0:T(1,128)S(1)}, f32[2,8,1,128]{3,2,1,0:T(1,128)S(1)}, u32[]{:S(2)}, u32[]{:S(2)}) collective-permute-start(f32[2,8,1,128]{3,2,1,0:T(1,128)S(1)} %slice.966), channel_id=1, source_target_pairs={{16,0},{17,1},{18,2},{19,3},{20,4},{21,5},{22,6},{23,7},{24,8},{25... | collective-permute-start | bytes 24584 | tf_op jit(solution)/shard_map/ppermute | solution.py:16
  3.1 5.4 %collective-permute-start.17 = (f32[2,1,32,128]{3,2,1,0:T(8,128)S(1)}, f32[2,1,32,128]{3,2,1,0:T(8,128)S(1)}, u32[]{:S(2)}, u32[]{:S(2)}) collective-permute-start(f32[2,1,32,128]{3,2,1,0:T(8,128)S(1)} %slice.971), channel_id=1, source_target_pairs={{1,0},{2,1},{3,2},{4,3},{5,4},{6,5},{7,6},{8,7},{9,8},{10,9},{11,1... | collective-permute-start | bytes 98312 | tf_op jit(solution)/shard_map/ppermute | solution.py:16
  4.4 5.8 %collective-permute-start = (f32[2,8,1,128]{3,2,1,0:T(1,128)S(1)}, f32[2,8,1,128]{3,2,1,0:T(1,128)S(1)}, u32[]{:S(2)}, u32[]{:S(2)}) collective-permute-start(f32[2,8,1,128]{3,2,1,0:T(1,128)S(1)} %slice.635), channel_id=1, source_target_pairs={{16,0},{17,1},{18,2},{19,3},{20,4},{21,5},{22,6},{23,7},{24,8},{25... | collective-permute-start | bytes 24584 | tf_op jit(solution)/shard_map/ppermute | solution.py:16
  5.7 4.5 %collective-permute-start.1 = (f32[2,1,32,128]{3,2,1,0:T(8,128)S(1)}, f32[2,1,32,128]{3,2,1,0:T(8,128)S(1)}, u32[]{:S(2)}, u32[]{:S(2)}) collective-permute-start(f32[2,1,32,128]{3,2,1,0:T(8,128)S(1)} %slice.640), channel_id=1, source_target_pairs={{1,0},{2,1},{3,2},{4,3},{5,4},{6,5},{7,6},{8,7},{9,8},{10,9},{11,1... | collective-permute-start | bytes 98312 | tf_op jit(solution)/shard_map/ppermute | solution.py:16
  7.1 0.9 copy-start.4
  8.6 1.0 copy-start.3
  10.3 1.0 copy-start.2
  11.5 17.6 %collective-permute-start.18 = (f32[2,8,1,128]{3,2,1,0:T(1,128)S(1)}, f32[2,8,1,128]{3,2,1,0:T(1,128)S(1)}, u32[]{:S(2)}, u32[]{:S(2)}) collective-permute-start(f32[2,8,1,128]{3,2,1,0:T(1,128)S(1)} %slice.982), channel_id=1, source_target_pairs={{0,16},{1,17},{2,18},{3,19},{4,20},{5,21},{6,22},{7,23},{8,24},{9,... | collective-permute-start | bytes 24584 | tf_op jit(solution)/shard_map/ppermute | solution.py:16
  15.8 13.2 %collective-permute-start.19 = (f32[2,1,32,128]{3,2,1,0:T(8,128)S(1)}, f32[2,1,32,128]{3,2,1,0:T(8,128)S(1)}, u32[]{:S(2)}, u32[]{:S(2)}) collective-permute-start(f32[2,1,32,128]{3,2,1,0:T(8,128)S(1)} %slice.987), channel_id=1, source_target_pairs={{0,1},{1,2},{2,3},{3,4},{4,5},{5,6},{6,7},{7,8},{8,9},{9,10},{10,1... | collective-permute-start | bytes 98312 | tf_op jit(solution)/shard_map/ppermute | solution.py:16
  20.5 4.9 %collective-permute-start.2 = (f32[2,8,1,128]{3,2,1,0:T(1,128)S(1)}, f32[2,8,1,128]{3,2,1,0:T(1,128)S(1)}, u32[]{:S(2)}, u32[]{:S(2)}) collective-permute-start(f32[2,8,1,128]{3,2,1,0:T(1,128)S(1)} %slice.854), channel_id=1, source_target_pairs={{0,16},{1,17},{2,18},{3,19},{4,20},{5,21},{6,22},{7,23},{8,24},{9,... | collective-permute-start | bytes 24584 | tf_op jit(solution)/shard_map/ppermute | solution.py:16
  22.1 3.9 %collective-permute-start.3 = (f32[2,1,32,128]{3,2,1,0:T(8,128)S(1)}, f32[2,1,32,128]{3,2,1,0:T(8,128)S(1)}, u32[]{:S(2)}, u32[]{:S(2)}) collective-permute-start(f32[2,1,32,128]{3,2,1,0:T(8,128)S(1)} %slice.859), channel_id=1, source_target_pairs={{0,1},{1,2},{2,3},{3,4},{4,5},{5,6},{6,7},{7,8},{8,9},{9,10},{10,1... | collective-permute-start | bytes 98312 | tf_op jit(solution)/shard_map/ppermute | solution.py:16
  26.3 5.5 %collective-permute-start.4 = (f32[2,8,1,128]{3,2,1,0:T(1,128)S(1)}, f32[2,8,1,128]{3,2,1,0:T(1,128)S(1)}, u32[]{:S(2)}, u32[]{:S(2)}) collective-permute-start(f32[2,8,1,128]{3,2,1,0:T(1,128)S(1)} %slice.870), channel_id=1, source_target_pairs={{16,0},{17,1},{18,2},{19,3},{20,4},{21,5},{22,6},{23,7},{24,8},{25... | collective-permute-start | bytes 24584 | tf_op jit(solution)/shard_map/ppermute | solution.py:16
  27.6 4.7 %collective-permute-start.5 = (f32[2,1,32,128]{3,2,1,0:T(8,128)S(1)}, f32[2,1,32,128]{3,2,1,0:T(8,128)S(1)}, u32[]{:S(2)}, u32[]{:S(2)}) collective-permute-start(f32[2,1,32,128]{3,2,1,0:T(8,128)S(1)} %slice.875), channel_id=1, source_target_pairs={{1,0},{2,1},{3,2},{4,3},{5,4},{6,5},{7,6},{8,7},{9,8},{10,9},{11,1... | collective-permute-start | bytes 98312 | tf_op jit(solution)/shard_map/ppermute | solution.py:16
  32.7 9.6 %collective-permute-start.6 = (f32[2,8,1,128]{3,2,1,0:T(1,128)S(1)}, f32[2,8,1,128]{3,2,1,0:T(1,128)S(1)}, u32[]{:S(2)}, u32[]{:S(2)}) collective-permute-start(f32[2,8,1,128]{3,2,1,0:T(1,128)S(1)} %slice.886), channel_id=1, source_target_pairs={{0,16},{1,17},{2,18},{3,19},{4,20},{5,21},{6,22},{7,23},{8,24},{9,... | collective-permute-start | bytes 24584 | tf_op jit(solution)/shard_map/ppermute | solution.py:16
  37.0 6.0 %collective-permute-start.7 = (f32[2,1,32,128]{3,2,1,0:T(8,128)S(1)}, f32[2,1,32,128]{3,2,1,0:T(8,128)S(1)}, u32[]{:S(2)}, u32[]{:S(2)}) collective-permute-start(f32[2,1,32,128]{3,2,1,0:T(8,128)S(1)} %slice.891), channel_id=1, source_target_pairs={{0,1},{1,2},{2,3},{3,4},{4,5},{5,6},{6,7},{7,8},{8,9},{9,10},{10,1... | collective-permute-start | bytes 98312 | tf_op jit(solution)/shard_map/ppermute | solution.py:16
  43.3 5.5 %collective-permute-start.8 = (f32[2,8,1,128]{3,2,1,0:T(1,128)S(1)}, f32[2,8,1,128]{3,2,1,0:T(1,128)S(1)}, u32[]{:S(2)}, u32[]{:S(2)}) collective-permute-start(f32[2,8,1,128]{3,2,1,0:T(1,128)S(1)} %slice.902), channel_id=1, source_target_pairs={{16,0},{17,1},{18,2},{19,3},{20,4},{21,5},{22,6},{23,7},{24,8},{25... | collective-permute-start | bytes 24584 | tf_op jit(solution)/shard_map/ppermute | solution.py:16
  44.6 4.2 %collective-permute-start.9 = (f32[2,1,32,128]{3,2,1,0:T(8,128)S(1)}, f32[2,1,32,128]{3,2,1,0:T(8,128)S(1)}, u32[]{:S(2)}, u32[]{:S(2)}) collective-permute-start(f32[2,1,32,128]{3,2,1,0:T(8,128)S(1)} %slice.907), channel_id=1, source_target_pairs={{1,0},{2,1},{3,2},{4,3},{5,4},{6,5},{7,6},{8,7},{9,8},{10,9},{11,1... | collective-permute-start | bytes 98312 | tf_op jit(solution)/shard_map/ppermute | solution.py:16
  49.2 8.4 %collective-permute-start.10 = (f32[2,8,1,128]{3,2,1,0:T(1,128)S(1)}, f32[2,8,1,128]{3,2,1,0:T(1,128)S(1)}, u32[]{:S(2)}, u32[]{:S(2)}) collective-permute-start(f32[2,8,1,128]{3,2,1,0:T(1,128)S(1)} %slice.918), channel_id=1, source_target_pairs={{0,16},{1,17},{2,18},{3,19},{4,20},{5,21},{6,22},{7,23},{8,24},{9,... | collective-permute-start | bytes 24584 | tf_op jit(solution)/shard_map/ppermute | solution.py:16
  52.7 5.6 %collective-permute-start.11 = (f32[2,1,32,128]{3,2,1,0:T(8,128)S(1)}, f32[2,1,32,128]{3,2,1,0:T(8,128)S(1)}, u32[]{:S(2)}, u32[]{:S(2)}) collective-permute-start(f32[2,1,32,128]{3,2,1,0:T(8,128)S(1)} %slice.923), channel_id=1, source_target_pairs={{0,1},{1,2},{2,3},{3,4},{4,5},{5,6},{6,7},{7,8},{8,9},{9,10},{10,1... | collective-permute-start | bytes 98312 | tf_op jit(solution)/shard_map/ppermute | solution.py:16
  58.7 5.5 %collective-permute-start.12 = (f32[2,8,1,128]{3,2,1,0:T(1,128)S(1)}, f32[2,8,1,128]{3,2,1,0:T(1,128)S(1)}, u32[]{:S(2)}, u32[]{:S(2)}) collective-permute-start(f32[2,8,1,128]{3,2,1,0:T(1,128)S(1)} %slice.934), channel_id=1, source_target_pairs={{16,0},{17,1},{18,2},{19,3},{20,4},{21,5},{22,6},{23,7},{24,8},{25... | collective-permute-start | bytes 24584 | tf_op jit(solution)/shard_map/ppermute | solution.py:16
  60.0 4.2 %collective-permute-start.13 = (f32[2,1,32,128]{3,2,1,0:T(8,128)S(1)}, f32[2,1,32,128]{3,2,1,0:T(8,128)S(1)}, u32[]{:S(2)}, u32[]{:S(2)}) collective-permute-start(f32[2,1,32,128]{3,2,1,0:T(8,128)S(1)} %slice.939), channel_id=1, source_target_pairs={{1,0},{2,1},{3,2},{4,3},{5,4},{6,5},{7,6},{8,7},{9,8},{10,9},{11,1... | collective-permute-start | bytes 98312 | tf_op jit(solution)/shard_map/ppermute | solution.py:16
  64.6 9.3 %copy-start.1 = (f32[3,8,32,128]{3,2,1,0:T(8,128)}, f32[3,8,32,128]{3,2,1,0:T(8,128)S(1)}, u32[]{:S(2)}) copy-start(f32[3,8,32,128]{3,2,1,0:T(8,128)S(1)} %fusion.3) | copy-start | bytes 1179652
  64.7 8.6 %collective-permute-start.14 = (f32[2,8,1,128]{3,2,1,0:T(1,128)S(1)}, f32[2,8,1,128]{3,2,1,0:T(1,128)S(1)}, u32[]{:S(2)}, u32[]{:S(2)}) collective-permute-start(f32[2,8,1,128]{3,2,1,0:T(1,128)S(1)} %slice.950), channel_id=1, source_target_pairs={{0,16},{1,17},{2,18},{3,19},{4,20},{5,21},{6,22},{7,23},{8,24},{9,... | collective-permute-start | bytes 24584 | tf_op jit(solution)/shard_map/ppermute | solution.py:16
  68.1 5.8 %collective-permute-start.15 = (f32[2,1,32,128]{3,2,1,0:T(8,128)S(1)}, f32[2,1,32,128]{3,2,1,0:T(8,128)S(1)}, u32[]{:S(2)}, u32[]{:S(2)}) collective-permute-start(f32[2,1,32,128]{3,2,1,0:T(8,128)S(1)} %slice.955), channel_id=1, source_target_pairs={{0,1},{1,2},{2,3},{3,4},{4,5},{5,6},{6,7},{7,8},{8,9},{9,10},{10,1... | collective-permute-start | bytes 98312 | tf_op jit(solution)/shard_map/ppermute | solution.py:16
  74.0 1.0 copy-start.5
  76.2 5.5 %collective-permute-start.20 = (f32[2,8,1,128]{3,2,1,0:T(1,128)S(1)}, f32[2,8,1,128]{3,2,1,0:T(1,128)S(1)}, u32[]{:S(2)}, u32[]{:S(2)}) collective-permute-start(f32[2,8,1,128]{3,2,1,0:T(1,128)S(1)} %slice.998), channel_id=1, source_target_pairs={{16,0},{17,1},{18,2},{19,3},{20,4},{21,5},{22,6},{23,7},{24,8},{25... | collective-permute-start | bytes 24584 | tf_op jit(solution)/shard_map/ppermute | solution.py:16
  77.5 4.2 %collective-permute-start.21 = (f32[2,1,32,128]{3,2,1,0:T(8,128)S(1)}, f32[2,1,32,128]{3,2,1,0:T(8,128)S(1)}, u32[]{:S(2)}, u32[]{:S(2)}) collective-permute-start(f32[2,1,32,128]{3,2,1,0:T(8,128)S(1)} %slice.1003), channel_id=1, source_target_pairs={{1,0},{2,1},{3,2},{4,3},{5,4},{6,5},{7,6},{8,7},{9,8},{10,9},{11,1... | collective-permute-start | bytes 98312 | tf_op jit(solution)/shard_map/ppermute | solution.py:16
  82.1 9.3 %collective-permute-start.22 = (f32[2,8,1,128]{3,2,1,0:T(1,128)S(1)}, f32[2,8,1,128]{3,2,1,0:T(1,128)S(1)}, u32[]{:S(2)}, u32[]{:S(2)}) collective-permute-start(f32[2,8,1,128]{3,2,1,0:T(1,128)S(1)} %slice.1014), channel_id=1, source_target_pairs={{0,16},{1,17},{2,18},{3,19},{4,20},{5,21},{6,22},{7,23},{8,24},{9,... | collective-permute-start | bytes 24584 | tf_op jit(solution)/shard_map/ppermute | solution.py:16
  85.5 6.5 %collective-permute-start.23 = (f32[2,1,32,128]{3,2,1,0:T(8,128)S(1)}, f32[2,1,32,128]{3,2,1,0:T(8,128)S(1)}, u32[]{:S(2)}, u32[]{:S(2)}) collective-permute-start(f32[2,1,32,128]{3,2,1,0:T(8,128)S(1)} %slice.1019), channel_id=1, source_target_pairs={{0,1},{1,2},{2,3},{3,4},{4,5},{5,6},{6,7},{7,8},{8,9},{9,10},{10,1... | collective-permute-start | bytes 98312 | tf_op jit(solution)/shard_map/ppermute | solution.py:16
  92.4 5.5 %collective-permute-start.24 = (f32[2,8,1,128]{3,2,1,0:T(1,128)S(1)}, f32[2,8,1,128]{3,2,1,0:T(1,128)S(1)}, u32[]{:S(2)}, u32[]{:S(2)}) collective-permute-start(f32[2,8,1,128]{3,2,1,0:T(1,128)S(1)} %slice.1030), channel_id=1, source_target_pairs={{16,0},{17,1},{18,2},{19,3},{20,4},{21,5},{22,6},{23,7},{24,8},{25... | collective-permute-start | bytes 24584 | tf_op jit(solution)/shard_map/ppermute | solution.py:16
  93.7 4.2 %collective-permute-start.25 = (f32[2,1,32,128]{3,2,1,0:T(8,128)S(1)}, f32[2,1,32,128]{3,2,1,0:T(8,128)S(1)}, u32[]{:S(2)}, u32[]{:S(2)}) collective-permute-start(f32[2,1,32,128]{3,2,1,0:T(8,128)S(1)} %slice.1035), channel_id=1, source_target_pairs={{1,0},{2,1},{3,2},{4,3},{5,4},{6,5},{7,6},{8,7},{9,8},{10,9},{11,1... | collective-permute-start | bytes 98312 | tf_op jit(solution)/shard_map/ppermute | solution.py:16
  98.3 9.3 %collective-permute-start.26 = (f32[2,8,1,128]{3,2,1,0:T(1,128)S(1)}, f32[2,8,1,128]{3,2,1,0:T(1,128)S(1)}, u32[]{:S(2)}, u32[]{:S(2)}) collective-permute-start(f32[2,8,1,128]{3,2,1,0:T(1,128)S(1)} %slice.1046), channel_id=1, source_target_pairs={{0,16},{1,17},{2,18},{3,19},{4,20},{5,21},{6,22},{7,23},{8,24},{9,... | collective-permute-start | bytes 24584 | tf_op jit(solution)/shard_map/ppermute | solution.py:16
  101.7 6.5 %collective-permute-start.27 = (f32[2,1,32,128]{3,2,1,0:T(8,128)S(1)}, f32[2,1,32,128]{3,2,1,0:T(8,128)S(1)}, u32[]{:S(2)}, u32[]{:S(2)}) collective-permute-start(f32[2,1,32,128]{3,2,1,0:T(8,128)S(1)} %slice.1051), channel_id=1, source_target_pairs={{0,1},{1,2},{2,3},{3,4},{4,5},{5,6},{6,7},{7,8},{8,9},{9,10},{10,1... | collective-permute-start | bytes 98312 | tf_op jit(solution)/shard_map/ppermute | solution.py:16
where the time goes:
time: 327 us; the launch traced here: 326 us
  other arithmetic  181 us (55%)
  starting transfers between devices  75.7 us (23%)
  blocking collectives  43.7 us (13%)
  waiting for transfers between devices  18.1 us (6%)
  local copies, waits for them, and re-layouts  5.17 us (2%)
    scatter-add x1, other arithmetic, local(): jax.ops.segment_sum(grad.reshape(-1), voxel_ids.reshape(-1), num_segments...  173 us
    ppermute x28, starting transfers between devices, passed_along(): lax.ppermute(value, axis, [(source, source + steps) for source in range(f...  75.7 us
    unnamed x1, blocking collectives  43.7 us
    ppermute x28, waiting for transfers between devices, passed_along(): lax.ppermute(value, axis, [(source, source + steps) for source in range(f...  18.1 us
  transfers between devices with their start and end apart: 28, of which 13 were waited for; matrix products, arithmetic and copies ran while one was open for 1% of the time, Pallas kernels for 0%

commit v1 on v0

v1 whole, which is shorter than its diff:
```python
import jax
import jax.numpy as jnp
from jax import lax
from jax.experimental import pallas as pl
from jax.experimental.pallas import tpu as pltpu
from jax.sharding import PartitionSpec as P

STEPS = 4
COURANT = 0.5
MESH = pl.DeviceIdType.MESH
VOX_DEV = 64
UNROLL = 1


def make_kernel(ng, nb, nx, nz, ny):
    n = ng * nb
    steps = STEPS
    lo_row, hi_row = 8, 8 + nz

    def kernel(e_in, h_in, eps_in, ce_in, ch_in, ids_in, e_out, h_out, v_out,
               E, H, G, AH, AE, CURL, eps, ids, h0, ah0, zs, zl, S, R, part,
               in_sem, out_sem, xs_sem, xr_sem, zs_sem, zr_sem, as_sem, ar_sem):
        grp = lax.axis_index("grp")
        blk = lax.axis_index("blk")
        me = grp * nb + blk
        lane = lax.broadcasted_iota(jnp.int32, (nz, ny), 1)

        loads = [
            pltpu.make_async_copy(ce_in, AE.at[0], in_sem.at[0]),
            pltpu.make_async_copy(eps_in, eps, in_sem.at[1]),
            pltpu.make_async_copy(e_in, E.at[0, :, 0:nx, 0:nz, :], in_sem.at[2]),
            pltpu.make_async_copy(h_in, h0, in_sem.at[3]),
            pltpu.make_async_copy(ch_in, ah0, in_sem.at[4]),
            pltpu.make_async_copy(ids_in, ids, in_sem.at[5]),
        ]
        for load in loads:
            load.start()

        barrier = pltpu.get_barrier_semaphore()

        @pl.loop(1, n)
        def _(j):
            other = (me + j) % n
            pl.semaphore_signal(barrier, inc=1, device_id=(other // nb, other % nb), device_id_type=MESH)

        @pl.when(blk == nb - 1)
        def _():
            E[0:steps, 1:3, nx, 0:nz, :] = jnp.zeros((steps, 2, nz, ny), jnp.float32)
            G[:, 1:3, nx, 0:nz, :] = jnp.zeros((steps - 1, 2, nz, ny), jnp.float32)

        @pl.when(blk == 0)
        def _():
            H[:, 1:3, 0, lo_row:hi_row, :] = jnp.zeros((steps, 2, nz, ny), jnp.float32)
            AH[:, 1:3, 0, lo_row:hi_row, :] = jnp.zeros((steps - 1, 2, nz, ny), jnp.float32)

        rounds = 4 * steps - 2
        for r in range(rounds):
            edge = ng - 1 if r % 2 == 0 else 0

            @pl.when(grp == edge)
            def _(r=r):
                zl[r] = jnp.zeros((2, nx, ny), jnp.float32)

        def xcopy(r, buf):
            if r % 2 == 0:
                src, dst, to = buf.at[1:3, 0, 0:nz, :], buf.at[1:3, nx, 0:nz, :], blk - 1
            else:
                src, dst, to = buf.at[1:3, nx, lo_row:hi_row, :], buf.at[1:3, 0, lo_row:hi_row, :], blk + 1
            return pltpu.make_async_remote_copy(src, dst, xs_sem.at[r], xr_sem.at[r], device_id=(grp, to), device_id_type=MESH)

        def zcopy(r):
            to = grp - 1 if r % 2 == 0 else grp + 1
            return pltpu.make_async_remote_copy(zs.at[r], zl.at[r], zs_sem.at[r], zr_sem.at[r], device_id=(to, blk), device_id_type=MESH)

        def x_sends(r):
            return blk > 0 if r % 2 == 0 else blk < nb - 1

        def x_gets(r):
            return blk < nb - 1 if r % 2 == 0 else blk > 0

        def z_sends(r):
            return grp > 0 if r % 2 == 0 else grp < ng - 1

        def z_gets(r):
            return grp < ng - 1 if r % 2 == 0 else grp > 0

        used = []

        def send(r, buf):
            used.append((r, buf))

            @pl.when(x_sends(r))
            def _():
                xcopy(r, buf).start()

            @pl.when(z_sends(r))
            def _():
                zcopy(r).start()

        def get_z(r, buf):
            @pl.when(z_gets(r))
            def _():
                zcopy(r).wait_recv()

            for c in range(2):
                for i in range(nx):
                    if r % 2 == 0:
                        buf[c, i, nz:nz + 1, :] = zl[r, c, i:i + 1, :]
                    else:
                        buf[c, i + 1, lo_row - 1:lo_row, :] = zl[r, c, i:i + 1, :]

        def get_x(r, buf):
            @pl.when(x_gets(r))
            def _():
                xcopy(r, buf).wait_recv()

        def curl_f(buf, i):
            vx, vy, vz = (buf[c, i, 0:nz, :] for c in range(3))

            def dy(v):
                return jnp.where(lane == ny - 1, 0.0, pltpu.roll(v, ny - 1, 1)) - v

            dxy, dxz = (buf[c, i + 1, 0:nz, :] - v for c, v in ((1, vy), (2, vz)))
            dzx, dzy = (buf[c, i, 1:nz + 1, :] - v for c, v in ((0, vx), (1, vy)))
            return dy(vz) - dzy, dzx - dxz, dxy - dy(vx)

        def curl_b(buf, i):
            vx, vy, vz = (buf[c, i + 1, lo_row:hi_row, :] for c in range(3))

            def dy(v):
                return v - jnp.where(lane == 0, 0.0, pltpu.roll(v, 1, 1))

            dxy, dxz = (v - buf[c, i, lo_row:hi_row, :] for c, v in ((1, vy), (2, vz)))
            dzx, dzy = (v - buf[c, i + 1, lo_row - 1:hi_row - 1, :] for c, v in ((0, vx), (1, vy)))
            return dy(vz) - dzy, dzx - dxz, dxy - dy(vx)

        def each(first, last, body):
            def step(i, carry):
                body(i)
                return carry
            lax.fori_loop(first, last, step, 0, unroll=UNROLL)

        def f_step(r_in, src, prev, dst, r_out, sign):
            def body(i):
                cv = curl_f(src, i)
                for c in range(3):
                    new = prev(c, i) + sign * cv[c]
                    dst[c, i + 1, lo_row:hi_row, :] = new
                    if c < 2:
                        zs[r_out, c, pl.ds(i, 1), :] = new[nz - 1:nz, :]

            get_z(r_in, src)
            each(0, nx - 1, body)
            get_x(r_in, src)
            body(nx - 1)
            send(r_out, dst)

        def b_step(r_in, src, body):
            get_z(r_in, src)
            each(1, nx, body)
            get_x(r_in, src)
            body(0)

        loads[0].wait()
        loads[1].wait()

        def first_g(i):
            for c in range(3):
                g = eps[i] * AE[0, c, i]
                G[0, c, i, 0:nz, :] = g
                if c < 2:
                    zs[2 * steps, c, pl.ds(i, 1), :] = g[0:1, :]

        each(0, nx, first_g)
        loads[2].wait()
        for c in range(2):
            for i in range(nx):
                zs[0, c, i:i + 1, :] = E[0, c, i, 0:1, :]
        pl.semaphore_wait(barrier, n - 1)
        send(0, E.at[0])
        send(2 * steps, G.at[0])
        for load in loads[3:]:
            load.wait()

        for k in range(steps):
            rf, ra = 2 * k, 2 * steps + 2 * k
            adj = k < steps - 1
            if k == 0:
                h_prev = lambda c, i: h0[c, i]
                a_prev = lambda c, i: ah0[c, i]
            else:
                h_prev = lambda c, i, k=k: H[k - 1, c, i + 1, lo_row:hi_row, :]
                a_prev = lambda c, i, k=k: AH[k - 1, c, i + 1, lo_row:hi_row, :]
            f_step(rf, E.at[k], h_prev, H.at[k], rf + 1, -COURANT)
            if not adj:
                h_copy = pltpu.make_async_copy(H.at[k, :, 1:nx + 1, lo_row:hi_row, :], h_out, out_sem.at[0])
                h_copy.start()
            if adj:
                f_step(ra, G.at[k], a_prev, AH.at[k], ra + 1, COURANT)

            def e_body(i, k=k, rf=rf):
                cv = curl_b(H.at[k], i)
                scale = COURANT * eps[i]
                for c in range(3):
                    CURL[k, c, i] = cv[c]
                    new = E[k, c, i, 0:nz, :] + scale * cv[c]
                    E[k + 1, c, i, 0:nz, :] = new
                    if c < 2 and k < steps - 1:
                        zs[rf + 2, c, pl.ds(i, 1), :] = new[0:1, :]

            b_step(rf + 1, H.at[k], e_body)
            if k < steps - 1:
                send(rf + 2, E.at[k + 1])
            else:
                e_copy = pltpu.make_async_copy(E.at[steps, :, 0:nx, 0:nz, :], e_out, out_sem.at[1])
                e_copy.start()
            if adj:
                def a_body(i, k=k, ra=ra):
                    cv = curl_b(AH.at[k], i)
                    scale = eps[i]
                    for c in range(3):
                        new = AE[k, c, i] - COURANT * cv[c]
                        AE[k + 1, c, i] = new
                        if k < steps - 2:
                            g = scale * new
                            G[k + 1, c, i, 0:nz, :] = g
                            if c < 2:
                                zs[ra + 2, c, pl.ds(i, 1), :] = g[0:1, :]

                b_step(ra + 1, AH.at[k], a_body)
                if k < steps - 2:
                    send(ra + 2, G.at[k + 1])

        own = lax.broadcasted_iota(jnp.int32, (n, ny), 0)
        place = lax.broadcasted_iota(jnp.int32, (VOX_DEV, ny), 0)
        part[...] = jnp.zeros_like(part)

        def seg(i):
            grad = jnp.zeros((nz, ny), jnp.float32)
            for k in range(steps):
                for c in range(3):
                    grad = grad + AE[steps - 1 - k, c, i] * CURL[k, c, i]
            grad = COURANT * grad
            coarse = grad.astype(jnp.bfloat16).astype(jnp.float32)
            fine = grad - coarse
            v = ids[i]
            high, low = v // VOX_DEV, v % VOX_DEV
            lhs, rhs = [], []
            for z in range(nz):
                hit = high[z:z + 1, :] == own
                lhs.append(jnp.concatenate([
                    jnp.where(hit, coarse[z:z + 1, :], 0.0).astype(jnp.bfloat16),
                    jnp.where(hit, fine[z:z + 1, :], 0.0).astype(jnp.bfloat16)], axis=0))
                rhs.append(jnp.where(low[z:z + 1, :] == place, 1.0, 0.0).astype(jnp.bfloat16))
            part[...] += lax.dot_general(
                jnp.concatenate(lhs, axis=1), jnp.concatenate(rhs, axis=1),
                (((1,), (1,)), ((), ())), preferred_element_type=jnp.float32)

        @pl.loop(0, nx)
        def _(i):
            seg(i)

        both = part[0:n, :] + part[n:2 * n, :]
        both = jnp.concatenate([both, jnp.zeros((n, 128 - VOX_DEV), jnp.float32)], axis=1)
        for d in range(n):
            S[d] = both[d:d + 1, :]

        @pl.loop(1, n)
        def _(j):
            to = (me + j) % n
            pltpu.make_async_remote_copy(
                S.at[to], R.at[me], as_sem, ar_sem,
                device_id=(to // nb, to % nb), device_id_type=MESH).start()

        R[me] = S[me]
        rest = pl.ds(0, n - 1)
        pltpu.make_async_copy(R.at[rest], R.at[rest], ar_sem).wait()
        v_out[...] = jnp.sum(R[...], axis=0)[:, 0:VOX_DEV]
        pltpu.make_async_copy(S.at[rest], S.at[rest], as_sem).wait()
        h_copy.wait()
        e_copy.wait()
        for r, buf in used:
            @pl.when(x_sends(r))
            def _(r=r, buf=buf):
                xcopy(r, buf).wait_send()

            @pl.when(z_sends(r))
            def _(r=r):
                zcopy(r).wait_send()

    return kernel


def solution(mesh):
    ng, nb = mesh.shape["grp"], mesh.shape["blk"]
    n = ng * nb

    def local(e_field, h_field, inv_eps, cot_e, cot_h, voxel_ids):
        _, nx, nz, ny = e_field.shape
        f32 = jnp.float32
        padded = (3, nx + 1, nz + 8, ny)
        plain = (3, nx, nz, ny)
        rounds = 4 * STEPS - 2
        dma = pltpu.SemaphoreType.DMA
        hbm = pl.BlockSpec(memory_space=pl.ANY)
        e_new, h_new, vox = pl.pallas_call(
            make_kernel(ng, nb, nx, nz, ny),
            out_shape=(
                jax.ShapeDtypeStruct(plain, f32),
                jax.ShapeDtypeStruct(plain, f32),
                jax.ShapeDtypeStruct((1, VOX_DEV), f32),
            ),
            in_specs=[hbm] * 6,
            out_specs=(hbm, hbm, pl.BlockSpec(memory_space=pltpu.VMEM)),
            scratch_shapes=[
                pltpu.VMEM((STEPS + 1,) + padded, f32),
                pltpu.VMEM((STEPS,) + padded, f32),
                pltpu.VMEM((STEPS - 1,) + padded, f32),
                pltpu.VMEM((STEPS - 1,) + padded, f32),
                pltpu.VMEM((STEPS,) + plain, f32),
                pltpu.VMEM((STEPS,) + plain, f32),
                pltpu.VMEM(plain[1:], f32),
                pltpu.VMEM(plain[1:], jnp.int32),
                pltpu.VMEM(plain, f32),
                pltpu.VMEM(plain, f32),
                pltpu.VMEM((rounds, 2, nx, ny), f32),
                pltpu.VMEM((rounds, 2, nx, ny), f32),
                pltpu.VMEM((n, 1, 128), f32),
                pltpu.VMEM((n, 1, 128), f32),
                pltpu.VMEM((2 * n, VOX_DEV), f32),
                dma((6,)), dma((2,)), dma((rounds,)), dma((rounds,)),
                dma((rounds,)), dma((rounds,)), dma, dma,
            ],
            compiler_params=pltpu.CompilerParams(
                collective_id=0, has_side_effects=True, vmem_limit_bytes=40 * 1024 * 1024),
        )(e_field, h_field, inv_eps, cot_e, cot_h, voxel_ids)
        return e_new, h_new, vox.reshape(VOX_DEV)

    field, cell = P(None, "blk", "grp", None), P("blk", "grp", None)
    return jax.shard_map(
        local, mesh=mesh,
        in_specs=(field, field, cell, field, field, cell),
        out_specs=(field, field, P(("grp", "blk"))),
        check_vma=False,
    )
```

time: 327 us -> 49.2 us (0.15)
  other arithmetic: 181 us -> 0 us
  starting transfers between devices: 75.7 us -> 0 us
  blocking collectives: 43.7 us -> 0 us
  Pallas kernels: 0 us -> 40.5 us
  waiting for transfers between devices: 18.1 us -> 0 us
    scatter-add x1 -> x0, other arithmetic: 173 us -> none  [local(): jax.ops.segment_sum(grad.reshape(-1), voxel_ids.reshape(-1), num_segments...]
    ppermute x28 -> x0, starting transfers between devices: 75.7 us -> none  [passed_along(): lax.ppermute(value, axis, [(source, source + steps) for source in range(f...]
    unnamed x1 -> x0, blocking collectives: 43.7 us -> none
    pallas_call x0 -> x1, Pallas kernels: none -> 40.5 us  [local(): pl.pallas_call(make_kernel(ng, nb, nx, nz, ny), out_shape=(jax.ShapeDtype...]
    ppermute x28 -> x0, waiting for transfers between devices: 18.1 us -> none  [passed_along(): lax.ppermute(value, axis, [(source, source + steps) for source in range(f...]
    sub x45 -> x0, other arithmetic: 3.97 us -> none  [the longest x7 0.95 us: curl_backward(): pair_xz - jnp.concatenate([jnp.zeros_like(pair_xz[:, :, :, :1]), pair_xz[...]
    unnamed x13 -> x15, local copies, waits for them, and re-layouts: 4.15 us -> 7.79 us
  transfers between devices with their start and end apart: 28 -> 0, of which waited for: 13 -> 0; matrix products, arithmetic and copies ran while one was open for 1% -> 0% of each run, Pallas kernels for 0% -> 0%
where the time goes in v1:
time: 49.2 us; the launch traced here: 48.9 us
  Pallas kernels  40.5 us (82%)
  local copies, waits for them, and re-layouts  7.79 us (16%)
  between operations  0.65 us (1%)
    pallas_call x1, Pallas kernels, local(): pl.pallas_call(make_kernel(ng, nb, nx, nz, ny), out_shape=(jax.ShapeDtype...  40.5 us
    unnamed x15, local copies, waits for them, and re-layouts  7.79 us

profile of v1, /device:TPU:0, one launch (start us, length us, event | category | flops | bytes accessed | tf_op | source)
XLA Modules:
  0.0 48.9 jit_solution(6995081845756931025)
XLA Ops:
  0.6 0.0 copy-start
  0.6 1.0 %copy-done = f32[3,8,32,128]{3,2,1,0:T(8,128)S(1)} copy-done((f32[3,8,32,128]{3,2,1,0:T(8,128)S(1)}, f32[3,8,32,128]{3,2,1,0:T(8,128)}, u32[]{:S(2)}) %copy-start) | copy-done | bytes 393240
  1.6 0.0 copy-start.1
  1.6 1.0 %copy-done.1 = f32[3,8,32,128]{3,2,1,0:T(8,128)S(1)} copy-done((f32[3,8,32,128]{3,2,1,0:T(8,128)S(1)}, f32[3,8,32,128]{3,2,1,0:T(8,128)}, u32[]{:S(2)}) %copy-start.1) | copy-done | bytes 393240
  2.6 0.0 copy-start.2
  2.6 1.0 %copy-done.2 = f32[3,8,32,128]{3,2,1,0:T(8,128)S(1)} copy-done((f32[3,8,32,128]{3,2,1,0:T(8,128)S(1)}, f32[3,8,32,128]{3,2,1,0:T(8,128)}, u32[]{:S(2)}) %copy-start.2) | copy-done | bytes 393240
  3.6 0.0 copy-start.3
  3.6 1.0 %copy-done.3 = f32[3,8,32,128]{3,2,1,0:T(8,128)S(1)} copy-done((f32[3,8,32,128]{3,2,1,0:T(8,128)S(1)}, f32[3,8,32,128]{3,2,1,0:T(8,128)}, u32[]{:S(2)}) %copy-start.3) | copy-done | bytes 393240
  4.6 0.0 copy-start.4
  4.6 0.9 %copy-done.4 = f32[8,32,128]{2,1,0:T(8,128)S(1)} copy-done((f32[8,32,128]{2,1,0:T(8,128)S(1)}, f32[8,32,128]{2,1,0:T(8,128)}, u32[]{:S(2)}) %copy-start.4) | copy-done | bytes 131096
  5.5 0.0 copy-start.5
  5.5 0.9 %copy-done.5 = s32[8,32,128]{2,1,0:T(8,128)S(1)} copy-done((s32[8,32,128]{2,1,0:T(8,128)S(1)}, s32[8,32,128]{2,1,0:T(8,128)}, u32[]{:S(2)}) %copy-start.5) | copy-done | bytes 131096
  6.4 40.5 %shard_map.85 = (f32[3,8,32,128]{3,2,1,0:T(8,128)S(1)}, f32[3,8,32,128]{3,2,1,0:T(8,128)S(1)}, f32[1,64]{1,0:T(1,128)S(1)}) custom-call(f32[3,8,32,128]{3,2,1,0:T(8,128)S(1)} %copy-done, f32[3,8,32,128]{3,2,1,0:T(8,128)S(1)} %copy-done.1, f32[8,32,128]{2,1,0:T(8,128)S(1)} %copy-done.4, f32[3,8,32,128]{3,2,1,0:T(8,128)S(1)} %copy-done.2, ...), custom_call_target="tpu_custom_call" | custom-call | tf_op jit(solution)/shard_map/pallas_call | solution.py:306
  46.9 0.7 %copy.12 = f32[3,8,32,128]{3,2,1,0:T(8,128)} copy(f32[3,8,32,128]{3,2,1,0:T(8,128)S(1)} %get-tuple-element.12) | data formatting | bytes 786432
  47.7 0.7 %copy.13 = f32[3,8,32,128]{3,2,1,0:T(8,128)} copy(f32[3,8,32,128]{3,2,1,0:T(8,128)S(1)} %get-tuple-element.13) | data formatting | bytes 786432
  48.4 0.5 %copy.14 = f32[64]{0:T(128)} copy(f32[64]{0:T(128)S(1)} %bitcast.1) | data formatting | bytes 512
Async XLA Ops:
  0.6 1.0 %copy-start = (f32[3,8,32,128]{3,2,1,0:T(8,128)S(1)}, f32[3,8,32,128]{3,2,1,0:T(8,128)}, u32[]{:S(2)}) copy-start(f32[3,8,32,128]{3,2,1,0:T(8,128)} %e_in.1) | copy-start | bytes 1179652
  1.6 1.0 %copy-start.1 = (f32[3,8,32,128]{3,2,1,0:T(8,128)S(1)}, f32[3,8,32,128]{3,2,1,0:T(8,128)}, u32[]{:S(2)}) copy-start(f32[3,8,32,128]{3,2,1,0:T(8,128)} %h_in.1) | copy-start | bytes 1179652
  2.6 1.0 %copy-start.2 = (f32[3,8,32,128]{3,2,1,0:T(8,128)S(1)}, f32[3,8,32,128]{3,2,1,0:T(8,128)}, u32[]{:S(2)}) copy-start(f32[3,8,32,128]{3,2,1,0:T(8,128)} %ce_in.1) | copy-start | bytes 1179652
  3.6 1.0 %copy-start.3 = (f32[3,8,32,128]{3,2,1,0:T(8,128)S(1)}, f32[3,8,32,128]{3,2,1,0:T(8,128)}, u32[]{:S(2)}) copy-start(f32[3,8,32,128]{3,2,1,0:T(8,128)} %ch_in.1) | copy-start | bytes 1179652
  4.6 0.9 %copy-start.4 = (f32[8,32,128]{2,1,0:T(8,128)S(1)}, f32[8,32,128]{2,1,0:T(8,128)}, u32[]{:S(2)}) copy-start(f32[8,32,128]{2,1,0:T(8,128)} %eps_in.1) | copy-start | bytes 393220
  5.5 0.9 %copy-start.5 = (s32[8,32,128]{2,1,0:T(8,128)S(1)}, s32[8,32,128]{2,1,0:T(8,128)}, u32[]{:S(2)}) copy-start(s32[8,32,128]{2,1,0:T(8,128)} %ids_in.1) | copy-start | bytes 393220

commit v2 on v1

--- a/solution.py
+++ b/solution.py
@@ -9,7 +9,7 @@
 COURANT = 0.5
 MESH = pl.DeviceIdType.MESH
 VOX_DEV = 64
-UNROLL = 1
+UNROLL = True
 
 
 def make_kernel(ng, nb, nx, nz, ny):
@@ -332,7 +332,7 @@
                 dma((rounds,)), dma((rounds,)), dma, dma,
             ],
             compiler_params=pltpu.CompilerParams(
-                collective_id=0, has_side_effects=True, vmem_limit_bytes=40 * 1024 * 1024),
+                collective_id=0, has_side_effects=True, vmem_limit_bytes=60 * 1024 * 1024),
         )(e_field, h_field, inv_eps, cot_e, cot_h, voxel_ids)
         return e_new, h_new, vox.reshape(VOX_DEV)
 

time: 49.2 us -> 41.6 us (0.85)
  local copies, waits for them, and re-layouts: 7.79 us -> 3.08 us
  Pallas kernels: 40.5 us -> 37.7 us
    unnamed x15 -> x7, local copies, waits for them, and re-layouts: 7.79 us -> 3.08 us
    pallas_call x1, Pallas kernels: 40.5 us -> 37.7 us  [local(): pl.pallas_call(make_kernel(ng, nb, nx, nz, ny), out_shape=(jax.ShapeDtype...]
where the time goes in v2:
time: 41.6 us; the launch traced here: 41.5 us
  Pallas kernels  37.7 us (91%)
  local copies, waits for them, and re-layouts  3.08 us (7%)
  between operations  0.65 us (2%)
    pallas_call x1, Pallas kernels, local(): pl.pallas_call(make_kernel(ng, nb, nx, nz, ny), out_shape=(jax.ShapeDtype...  37.7 us
    unnamed x7, local copies, waits for them, and re-layouts  3.08 us

profile of v2, /device:TPU:0, one launch (start us, length us, event | category | flops | bytes accessed | tf_op | source)
XLA Modules:
  0.0 41.5 jit_solution(4064316836884921504)
XLA Ops:
  0.6 37.7 %shard_map.85 = (f32[3,8,32,128]{3,2,1,0:T(8,128)}, f32[3,8,32,128]{3,2,1,0:T(8,128)}, f32[1,64]{1,0:T(1,128)}) custom-call(f32[3,8,32,128]{3,2,1,0:T(8,128)} %e_in.1, f32[3,8,32,128]{3,2,1,0:T(8,128)} %h_in.1, f32[8,32,128]{2,1,0:T(8,128)} %eps_in.1, f32[3,8,32,128]{3,2,1,0:T(8,128)} %ce_in.1, f32[3,8,32,128]{3,2,1,0:T(8,128)} %ch_in.1, s32[8,32,128]{2,1,0:T(8,128)} %ids_in.1), custom_call_target="tpu_custom_call" | custom-call | tf_op jit(solution)/shard_map/pallas_call | solution.py:306
  38.4 0.0 copy-start
  38.4 1.8 %copy.12 = f32[3,8,32,128]{3,2,1,0:T(8,128)} copy(f32[3,8,32,128]{3,2,1,0:T(8,128)} %get-tuple-element.12) | data formatting | bytes 786432
  40.2 0.0 copy-done
  40.2 0.0 copy-start.1
  40.2 0.7 %copy.13 = f32[3,8,32,128]{3,2,1,0:T(8,128)} copy(f32[3,8,32,128]{3,2,1,0:T(8,128)S(1)} %copy-done) | data formatting | bytes 786432
  41.0 0.0 copy-done.1
  41.0 0.5 %copy.14 = f32[64]{0:T(128)} copy(f32[64]{0:T(128)S(1)} %bitcast.1) | data formatting | bytes 512
Async XLA Ops:
  38.4 1.8 %copy-start = (f32[3,8,32,128]{3,2,1,0:T(8,128)S(1)}, f32[3,8,32,128]{3,2,1,0:T(8,128)}, u32[]{:S(2)}) copy-start(f32[3,8,32,128]{3,2,1,0:T(8,128)} %get-tuple-element.13) | copy-start | bytes 1179652
  40.2 0.8 %copy-start.1 = (f32[1,64]{1,0:T(1,128)S(1)}, f32[1,64]{1,0:T(1,128)}, u32[]{:S(2)}) copy-start(f32[1,64]{1,0:T(1,128)} %get-tuple-element.8) | copy-start | bytes 772

commit v3 on v2

v3 whole, which is shorter than its diff:
```python
import jax
import jax.numpy as jnp
from jax import lax
from jax.experimental import pallas as pl
from jax.experimental.pallas import tpu as pltpu
from jax.sharding import PartitionSpec as P

STEPS = 4
COURANT = 0.5
MESH = pl.DeviceIdType.MESH
VOX_DEV = 64
UNROLL = True


def make_kernel(ng, nb, nx, nz, ny):
    n = ng * nb
    steps = STEPS
    top, end = 8, 8 + nz

    def kernel(e_in, h_in, eps_in, ce_in, ch_in, ids_in, e_out, h_out, v_out,
               E, H, G, AH, AE, CURL, eps, ids, zs_dn, zl_dn, zs_up, zl_up, cl_a, cl_b, zs_h, zl_h,
               S, R, part, in_sem, out_sem, as_sem, ar_sem, *link_sems):
        xd, xu, zd, zu, ca, cb, hx, hz = (link_sems[2 * j:2 * j + 2] for j in range(8))
        grp = lax.axis_index("grp")
        blk = lax.axis_index("blk")
        me = grp * nb + blk
        lane = lax.broadcasted_iota(jnp.int32, (nz, ny), 1)
        lane_h = lax.broadcasted_iota(jnp.int32, (end, ny), 1)

        loads = [
            pltpu.make_async_copy(ce_in, AE.at[0], in_sem.at[0]),
            pltpu.make_async_copy(eps_in, eps, in_sem.at[1]),
            pltpu.make_async_copy(e_in, E.at[0, :, 1:nx + 1, top:end, :], in_sem.at[2]),
            pltpu.make_async_copy(h_in, H.at[0, :, 1:nx + 1, top:end, :], in_sem.at[3]),
            pltpu.make_async_copy(ch_in, AH.at[0, :, 1:nx + 1, top:end, :], in_sem.at[4]),
            pltpu.make_async_copy(ids_in, ids, in_sem.at[5]),
        ]
        for load in loads:
            load.start()

        barrier = pltpu.get_barrier_semaphore()

        @pl.loop(1, n)
        def _(j):
            other = (me + j) % n
            pl.semaphore_signal(barrier, inc=1, device_id=(other // nb, other % nb), device_id_type=MESH)

        first_x, last_x = blk == 0, blk == nb - 1
        first_z, last_z = grp == 0, grp == ng - 1
        rounds = 2 * steps - 1

        @pl.when(last_x)
        def _():
            E[0:steps, 1:3, nx + 1, top:end, :] = jnp.zeros((steps, 2, nz, ny), jnp.float32)
            G[:, 1:3, nx + 1, top:end, :] = jnp.zeros((steps - 1, 2, nz, ny), jnp.float32)

        @pl.when(first_x)
        def _():
            H[:, 1:3, 0, top:end, :] = jnp.zeros((steps + 1, 2, nz, ny), jnp.float32)
            AH[:, 1:3, 0, top:end, :] = jnp.zeros((steps, 2, nz, ny), jnp.float32)

        @pl.when(last_z)
        def _():
            zl_dn[...] = jnp.zeros_like(zl_dn)

        @pl.when(jnp.logical_or(last_z, first_x))
        def _():
            cl_a[...] = jnp.zeros_like(cl_a)

        @pl.when(jnp.logical_or(first_z, last_x))
        def _():
            cl_b[...] = jnp.zeros_like(cl_b)

        def remote(src, dst, sems, r, to):
            return pltpu.make_async_remote_copy(src, dst, sems[0].at[r], sems[1].at[r], device_id=to, device_id_type=MESH)

        def links(r, buf):
            yes_dn, yes_up = jnp.logical_not(first_x), jnp.logical_not(last_x)
            z_dn, z_up = jnp.logical_not(first_z), jnp.logical_not(last_z)
            both = jnp.logical_and
            return [
                (yes_dn, yes_up, remote(buf.at[1:3, 1, top:end, :], buf.at[1:3, nx + 1, top:end, :], xd, r, (grp, blk - 1))),
                (yes_up, yes_dn, remote(buf.at[:, nx, top:end, :], buf.at[:, 0, top:end, :], xu, r, (grp, blk + 1))),
                (z_dn, z_up, remote(zs_dn.at[r], zl_dn.at[r], zd, r, (grp - 1, blk))),
                (z_up, z_dn, remote(zs_up.at[r], zl_up.at[r], zu, r, (grp + 1, blk))),
                (both(z_dn, yes_up), both(z_up, yes_dn), remote(zs_dn.at[r, 0, nx - 1], cl_a.at[r], ca, r, (grp - 1, blk + 1))),
                (both(z_up, yes_dn), both(z_dn, yes_up), remote(zs_up.at[r, 2, 0], cl_b.at[r], cb, r, (grp + 1, blk - 1))),
            ]

        def start_links(r, buf, h0=None):
            jobs = [links(r, buf), hlinks(r, h0) if h0 is not None else []]
            for sends, _, copy in jobs[0] + jobs[1]:
                used.append((sends, copy))
                pl.when(sends)(copy.start)

        def hlinks(r, h0):
            q = 0 if r == 0 else 1
            return [
                (jnp.logical_not(last_x), jnp.logical_not(first_x), remote(h0.at[1:3, nx, top:end, :], h0.at[1:3, 0, top:end, :], hx, q, (grp, blk + 1))),
                (jnp.logical_not(last_z), jnp.logical_not(first_z), remote(zs_h.at[q], zl_h.at[q], hz, q, (grp + 1, blk))),
            ]

        used = []

        def finish_links(r, buf, h0=None):
            jobs = links(r, buf) + (hlinks(r, h0) if h0 is not None else [])
            for _, gets, copy in jobs:
                pl.when(gets)(copy.wait_recv)
            for c in range(2):
                for i in range(nx):
                    buf[c, i + 1, end:end + 1, :] = zl_dn[r, c, i]
            buf[0, 0, end:end + 1, :] = cl_a[r]
            buf[2, nx + 1, top - 1:top, :] = cl_b[r]

            @pl.when(jnp.logical_not(first_z))
            def _():
                for c in range(3):
                    for i in range(nx):
                        buf[c, i + 1, top - 1:top, :] = zl_up[r, c, i]
                if h0 is not None:
                    for c in range(2):
                        for i in range(nx):
                            h0[c, i + 1, top - 1:top, :] = zl_h[0 if r == 0 else 1, c, i]

        def curl_f(buf, i):
            vx, vy, vz = (buf[c, i, 0:end, :] for c in range(3))

            def dy(v):
                return jnp.where(lane_h == ny - 1, 0.0, pltpu.roll(v, ny - 1, 1)) - v

            dxy, dxz = (buf[c, i + 1, 0:end, :] - v for c, v in ((1, vy), (2, vz)))
            dzx, dzy = (buf[c, i, 1:end + 1, :] - v for c, v in ((0, vx), (1, vy)))
            return dy(vz) - dzy, dzx - dxz, dxy - dy(vx)

        def curl_b(buf, i):
            vx, vy, vz = (buf[c, i, top:end, :] for c in range(3))

            def dy(v):
                return v - jnp.where(lane == 0, 0.0, pltpu.roll(v, 1, 1))

            dxy, dxz = (v - buf[c, i - 1, top:end, :] for c, v in ((1, vy), (2, vz)))
            dzx, dzy = (v - buf[c, i, top - 1:end - 1, :] for c, v in ((0, vx), (1, vy)))
            return dy(vz) - dzy, dzx - dxz, dxy - dy(vx)

        def each(first, last, body):
            def step(i, carry):
                body(i)
                return carry
            lax.fori_loop(first, last, step, 0, unroll=UNROLL)

        def f_step(src, prev, dst, sign):
            def body(i):
                cv = curl_f(src, i)
                for c in range(3):
                    dst[c, i, 0:end, :] = prev[c, i, 0:end, :] + sign * cv[c]

            @pl.when(jnp.logical_not(first_x))
            def _():
                vx, vy, vz = (src[c, 0, top:end, :] for c in range(3))

                def dy(v):
                    return jnp.where(lane == ny - 1, 0.0, pltpu.roll(v, ny - 1, 1)) - v

                cy = (src[0, 0, top + 1:end + 1, :] - vx) - (src[2, 1, top:end, :] - vz)
                cz = (src[1, 1, top:end, :] - vy) - dy(vx)
                dst[1, 0, top:end, :] = prev[1, 0, top:end, :] + sign * cy
                dst[2, 0, top:end, :] = prev[2, 0, top:end, :] + sign * cz

            each(1, nx + 1, body)

            @pl.when(first_z)
            def _():
                for c in range(2):
                    for i in range(1, nx + 1):
                        dst[c, i, top - 1:top, :] = jnp.zeros((1, ny), jnp.float32)

        def edge_rows(r, c, i, new):
            if c < 2:
                zs_dn[r, c, i - 1] = new[0:1, :]
            zs_up[r, c, i - 1] = new[nz - 1:nz, :]

        ra = steps
        loads[0].wait()
        loads[1].wait()

        def first_g(i):
            for c in range(3):
                g = eps[i - 1] * AE[0, c, i - 1]
                G[0, c, i, top:end, :] = g
                edge_rows(ra, c, i, g)

        each(1, nx + 1, first_g)
        for load in loads[2:5]:
            load.wait()
        for i in range(1, nx + 1):
            for c in range(3):
                edge_rows(0, c, i, E[0, c, i, top:end, :])
            for c in range(2):
                zs_h[0, c, i - 1] = H[0, c, i, end - 1:end, :]
                zs_h[1, c, i - 1] = AH[0, c, i, end - 1:end, :]
        pl.semaphore_wait(barrier, n - 1)
        start_links(0, E.at[0], H.at[0])
        start_links(ra, G.at[0], AH.at[0])
        loads[5].wait()

        for k in range(steps):
            finish_links(k, E.at[k], H.at[0] if k == 0 else None)
            f_step(E.at[k], H.at[k], H.at[k + 1], -COURANT)
            if k == steps - 1:
                h_copy = pltpu.make_async_copy(H.at[steps, :, 1:nx + 1, top:end, :], h_out, out_sem.at[0])
                h_copy.start()

            def e_body(i, k=k):
                cv = curl_b(H.at[k + 1], i)
                scale = COURANT * eps[i - 1]
                for c in range(3):
                    CURL[k, c, i - 1] = cv[c]
                    new = E[k, c, i, top:end, :] + scale * cv[c]
                    E[k + 1, c, i, top:end, :] = new
                    if k < steps - 1:
                        edge_rows(k + 1, c, i, new)

            each(1, nx + 1, e_body)
            if k == steps - 1:
                e_copy = pltpu.make_async_copy(E.at[steps, :, 1:nx + 1, top:end, :], e_out, out_sem.at[1])
                e_copy.start()
                continue
            start_links(k + 1, E.at[k + 1])
            finish_links(ra + k, G.at[k], AH.at[0] if k == 0 else None)
            f_step(G.at[k], AH.at[k], AH.at[k + 1], COURANT)

            def a_body(i, k=k):
                cv = curl_b(AH.at[k + 1], i)
                for c in range(3):
                    new = AE[k, c, i - 1] - COURANT * cv[c]
                    AE[k + 1, c, i - 1] = new
                    if k < steps - 2:
                        g = eps[i - 1] * new
                        G[k + 1, c, i, top:end, :] = g
                        edge_rows(ra + k + 1, c, i, g)

            each(1, nx + 1, a_body)
            if k < steps - 2:
                start_links(ra + k + 1, G.at[k + 1])

        own = lax.broadcasted_iota(jnp.int32, (n, ny), 0)
        place = lax.broadcasted_iota(jnp.int32, (VOX_DEV, ny), 0)
        part[...] = jnp.zeros_like(part)

        def seg(i):
            grad = jnp.zeros((nz, ny), jnp.float32)
            for k in range(steps):
                for c in range(3):
                    grad = grad + AE[steps - 1 - k, c, i] * CURL[k, c, i]
            grad = COURANT * grad
            coarse = grad.astype(jnp.bfloat16).astype(jnp.float32)
            fine = grad - coarse
            v = ids[i]
            high, low = v // VOX_DEV, v % VOX_DEV
            lhs, rhs = [], []
            for z in range(nz):
                hit = high[z:z + 1, :] == own
                lhs.append(jnp.concatenate([
                    jnp.where(hit, coarse[z:z + 1, :], 0.0).astype(jnp.bfloat16),
                    jnp.where(hit, fine[z:z + 1, :], 0.0).astype(jnp.bfloat16)], axis=0))
                rhs.append(jnp.where(low[z:z + 1, :] == place, 1.0, 0.0).astype(jnp.bfloat16))
            part[...] += lax.dot_general(
                jnp.concatenate(lhs, axis=1), jnp.concatenate(rhs, axis=1),
                (((1,), (1,)), ((), ())), preferred_element_type=jnp.float32)

        @pl.loop(0, nx)
        def _(i):
            seg(i)

        both = part[0:n, :] + part[n:2 * n, :]
        both = jnp.concatenate([both, jnp.zeros((n, 128 - VOX_DEV), jnp.float32)], axis=1)
        for d in range(n):
            S[d] = both[d:d + 1, :]

        @pl.loop(1, n)
        def _(j):
            to = (me + j) % n
            pltpu.make_async_remote_copy(
                S.at[to], R.at[me], as_sem, ar_sem,
                device_id=(to // nb, to % nb), device_id_type=MESH).start()

        R[me] = S[me]
        rest = pl.ds(0, n - 1)
        pltpu.make_async_copy(R.at[rest], R.at[rest], ar_sem).wait()
        v_out[...] = jnp.sum(R[...], axis=0)[:, 0:VOX_DEV]
        pltpu.make_async_copy(S.at[rest], S.at[rest], as_sem).wait()
        h_copy.wait()
        e_copy.wait()
        for sends, copy in used:
            pl.when(sends)(copy.wait_send)

    return kernel


def solution(mesh):
    ng, nb = mesh.shape["grp"], mesh.shape["blk"]
    n = ng * nb

    def local(e_field, h_field, inv_eps, cot_e, cot_h, voxel_ids):
        _, nx, nz, ny = e_field.shape
        f32 = jnp.float32
        padded = (3, nx + 2, nz + 16, ny)
        plain = (3, nx, nz, ny)
        rounds = 2 * STEPS - 1
        dma = pltpu.SemaphoreType.DMA
        hbm = pl.BlockSpec(memory_space=pl.ANY)
        e_new, h_new, vox = pl.pallas_call(
            make_kernel(ng, nb, nx, nz, ny),
            out_shape=(
                jax.ShapeDtypeStruct(plain, f32),
                jax.ShapeDtypeStruct(plain, f32),
                jax.ShapeDtypeStruct((1, VOX_DEV), f32),
            ),
            in_specs=[hbm] * 6,
            out_specs=(hbm, hbm, pl.BlockSpec(memory_space=pltpu.VMEM)),
            scratch_shapes=[
                pltpu.VMEM((STEPS + 1,) + padded, f32),
                pltpu.VMEM((STEPS + 1,) + padded, f32),
                pltpu.VMEM((STEPS - 1,) + padded, f32),
                pltpu.VMEM((STEPS,) + padded, f32),
                pltpu.VMEM((STEPS,) + plain, f32),
                pltpu.VMEM((STEPS,) + plain, f32),
                pltpu.VMEM(plain[1:], f32),
                pltpu.VMEM(plain[1:], jnp.int32),
                pltpu.VMEM((rounds, 2, nx, 1, ny), f32),
                pltpu.VMEM((rounds, 2, nx, 1, ny), f32),
                pltpu.VMEM((rounds, 3, nx, 1, ny), f32),
                pltpu.VMEM((rounds, 3, nx, 1, ny), f32),
                pltpu.VMEM((rounds, 1, ny), f32),
                pltpu.VMEM((rounds, 1, ny), f32),
                pltpu.VMEM((2, 2, nx, 1, ny), f32),
                pltpu.VMEM((2, 2, nx, 1, ny), f32),
                pltpu.VMEM((n, 1, 128), f32),
                pltpu.VMEM((n, 1, 128), f32),
                pltpu.VMEM((2 * n, VOX_DEV), f32),
                dma((6,)), dma((2,)), dma, dma,
            ] + [dma((rounds,))] * 12 + [dma((2,))] * 4,
            compiler_params=pltpu.CompilerParams(
                collective_id=0, has_side_effects=True, vmem_limit_bytes=60 * 1024 * 1024),
        )(e_field, h_field, inv_eps, cot_e, cot_h, voxel_ids)
        return e_new, h_new, vox.reshape(VOX_DEV)

    field, cell = P(None, "blk", "grp", None), P("blk", "grp", None)
    return jax.shard_map(
        local, mesh=mesh,
        in_specs=(field, field, cell, field, field, cell),
        out_specs=(field, field, P(("grp", "blk"))),
        check_vma=False,
    )
```

time: 41.6 us -> 33.2 us (0.80)
  Pallas kernels: 37.7 us -> 29.3 us
    pallas_call x1, Pallas kernels: 37.7 us -> 29.3 us  [local(): pl.pallas_call(make_kernel(ng, nb, nx, nz, ny), out_shape=(jax.ShapeDtype...]
where the time goes in v3:
time: 33.2 us; the launch traced here: 33 us
  Pallas kernels  29.3 us (88%)
  local copies, waits for them, and re-layouts  3.08 us (9%)
  between operations  0.65 us (2%)
    pallas_call x1, Pallas kernels, local(): pl.pallas_call(make_kernel(ng, nb, nx, nz, ny), out_shape=(jax.ShapeDtype...  29.3 us
    unnamed x7, local copies, waits for them, and re-layouts  3.08 us

profile of v3, /device:TPU:0, one launch (start us, length us, event | category | flops | bytes accessed | tf_op | source)
XLA Modules:
  0.0 33.0 jit_solution(17440369750274977372)
XLA Ops:
  0.6 29.3 %shard_map.85 = (f32[3,8,32,128]{3,2,1,0:T(8,128)}, f32[3,8,32,128]{3,2,1,0:T(8,128)}, f32[1,64]{1,0:T(1,128)}) custom-call(f32[3,8,32,128]{3,2,1,0:T(8,128)} %e_in.1, f32[3,8,32,128]{3,2,1,0:T(8,128)} %h_in.1, f32[8,32,128]{2,1,0:T(8,128)} %eps_in.1, f32[3,8,32,128]{3,2,1,0:T(8,128)} %ce_in.1, f32[3,8,32,128]{3,2,1,0:T(8,128)} %ch_in.1, s32[8,32,128]{2,1,0:T(8,128)} %ids_in.1), custom_call_target="tpu_custom_call" | custom-call | tf_op jit(solution)/shard_map/pallas_call | solution.py:312
  29.9 0.0 copy-start
  30.0 1.8 %copy.12 = f32[3,8,32,128]{3,2,1,0:T(8,128)} copy(f32[3,8,32,128]{3,2,1,0:T(8,128)} %get-tuple-element.12) | data formatting | bytes 786432
  31.8 0.0 copy-done
  31.8 0.0 copy-start.1
  31.8 0.7 %copy.13 = f32[3,8,32,128]{3,2,1,0:T(8,128)} copy(f32[3,8,32,128]{3,2,1,0:T(8,128)S(1)} %copy-done) | data formatting | bytes 786432
  32.5 0.0 copy-done.1
  32.5 0.5 %copy.14 = f32[64]{0:T(128)} copy(f32[64]{0:T(128)S(1)} %bitcast.1) | data formatting | bytes 512
Async XLA Ops:
  29.9 1.8 %copy-start = (f32[3,8,32,128]{3,2,1,0:T(8,128)S(1)}, f32[3,8,32,128]{3,2,1,0:T(8,128)}, u32[]{:S(2)}) copy-start(f32[3,8,32,128]{3,2,1,0:T(8,128)} %get-tuple-element.13) | copy-start | bytes 1179652
  31.8 0.8 %copy-start.1 = (f32[1,64]{1,0:T(1,128)S(1)}, f32[1,64]{1,0:T(1,128)}, u32[]{:S(2)}) copy-start(f32[1,64]{1,0:T(1,128)} %get-tuple-element.8) | copy-start | bytes 772

commit v4 on v3

--- a/solution.py
+++ b/solution.py
@@ -35,8 +35,8 @@
             pltpu.make_async_copy(ch_in, AH.at[0, :, 1:nx + 1, top:end, :], in_sem.at[4]),
             pltpu.make_async_copy(ids_in, ids, in_sem.at[5]),
         ]
-        for load in loads:
-            load.start()
+        for j in (2, 3, 0, 1, 4, 5):
+            loads[j].start()
 
         barrier = pltpu.get_barrier_semaphore()
 
@@ -87,8 +87,8 @@
                 (both(z_up, yes_dn), both(z_dn, yes_up), remote(zs_up.at[r, 2, 0], cl_b.at[r], cb, r, (grp + 1, blk - 1))),
             ]
 
-        def start_links(r, buf, h0=None):
-            jobs = [links(r, buf), hlinks(r, h0) if h0 is not None else []]
+        def start_links(r, buf, h0=None, part_of=slice(None)):
+            jobs = [links(r, buf)[part_of], hlinks(r, h0) if h0 is not None else []]
             for sends, _, copy in jobs[0] + jobs[1]:
                 used.append((sends, copy))
                 pl.when(sends)(copy.start)
@@ -180,6 +180,16 @@
             zs_up[r, c, i - 1] = new[nz - 1:nz, :]
 
         ra = steps
+        loads[2].wait()
+        for i in range(1, nx + 1):
+            for c in range(3):
+                edge_rows(0, c, i, E[0, c, i, top:end, :])
+        loads[3].wait()
+        for i in range(1, nx + 1):
+            for c in range(2):
+                zs_h[0, c, i - 1] = H[0, c, i, end - 1:end, :]
+        pl.semaphore_wait(barrier, n - 1)
+        start_links(0, E.at[0], H.at[0])
         loads[0].wait()
         loads[1].wait()
 
@@ -190,16 +200,10 @@
                 edge_rows(ra, c, i, g)
 
         each(1, nx + 1, first_g)
-        for load in loads[2:5]:
-            load.wait()
+        loads[4].wait()
         for i in range(1, nx + 1):
-            for c in range(3):
-                edge_rows(0, c, i, E[0, c, i, top:end, :])
             for c in range(2):
-                zs_h[0, c, i - 1] = H[0, c, i, end - 1:end, :]
                 zs_h[1, c, i - 1] = AH[0, c, i, end - 1:end, :]
-        pl.semaphore_wait(barrier, n - 1)
-        start_links(0, E.at[0], H.at[0])
         start_links(ra, G.at[0], AH.at[0])
         loads[5].wait()
 
@@ -220,12 +224,16 @@
                     if k < steps - 1:
                         edge_rows(k + 1, c, i, new)
 
-            each(1, nx + 1, e_body)
+            e_body(1)
+            e_body(nx)
+            if k < steps - 1:
+                start_links(k + 1, E.at[k + 1], part_of=slice(0, 2))
+            each(2, nx, e_body)
             if k == steps - 1:
                 e_copy = pltpu.make_async_copy(E.at[steps, :, 1:nx + 1, top:end, :], e_out, out_sem.at[1])
                 e_copy.start()
                 continue
-            start_links(k + 1, E.at[k + 1])
+            start_links(k + 1, E.at[k + 1], part_of=slice(2, 6))
             finish_links(ra + k, G.at[k], AH.at[0] if k == 0 else None)
             f_step(G.at[k], AH.at[k], AH.at[k + 1], COURANT)
 
@@ -239,9 +247,13 @@
                         G[k + 1, c, i, top:end, :] = g
                         edge_rows(ra + k + 1, c, i, g)
 
-            each(1, nx + 1, a_body)
+            a_body(1)
+            a_body(nx)
             if k < steps - 2:
-                start_links(ra + k + 1, G.at[k + 1])
+                start_links(ra + k + 1, G.at[k + 1], part_of=slice(0, 2))
+            each(2, nx, a_body)
+            if k < steps - 2:
+                start_links(ra + k + 1, G.at[k + 1], part_of=slice(2, 6))
 
         own = lax.broadcasted_iota(jnp.int32, (n, ny), 0)
         place = lax.broadcasted_iota(jnp.int32, (VOX_DEV, ny), 0)
@@ -268,9 +280,7 @@
                 jnp.concatenate(lhs, axis=1), jnp.concatenate(rhs, axis=1),
                 (((1,), (1,)), ((), ())), preferred_element_type=jnp.float32)
 
-        @pl.loop(0, nx)
-        def _(i):
-            seg(i)
+        lax.fori_loop(0, nx, lambda i, carry: (seg(i), carry)[1], 0, unroll=UNROLL)
 
         both = part[0:n, :] + part[n:2 * n, :]
         both = jnp.concatenate([both, jnp.zeros((n, 128 - VOX_DEV), jnp.float32)], axis=1)

time: 33.2 us -> 32.3 us (0.973)
  Pallas kernels: 29.3 us -> 28.4 us
    pallas_call x1, Pallas kernels: 29.3 us -> 28.4 us  [local(): pl.pallas_call(make_kernel(ng, nb, nx, nz, ny), out_shape=(jax.ShapeDtype...]
where the time goes in v4:
time: 32.3 us; the launch traced here: 32.1 us
  Pallas kernels  28.4 us (88%)
  local copies, waits for them, and re-layouts  3.08 us (10%)
  between operations  0.65 us (2%)
    pallas_call x1, Pallas kernels, local(): pl.pallas_call(make_kernel(ng, nb, nx, nz, ny), out_shape=(jax.ShapeDtype...  28.4 us
    unnamed x7, local copies, waits for them, and re-layouts  3.08 us

profile of v4, /device:TPU:0, one launch (start us, length us, event | category | flops | bytes accessed | tf_op | source)
XLA Modules:
  0.0 32.1 jit_solution(220304746134371318)
XLA Ops:
  0.6 28.4 %shard_map.85 = (f32[3,8,32,128]{3,2,1,0:T(8,128)}, f32[3,8,32,128]{3,2,1,0:T(8,128)}, f32[1,64]{1,0:T(1,128)}) custom-call(f32[3,8,32,128]{3,2,1,0:T(8,128)} %e_in.1, f32[3,8,32,128]{3,2,1,0:T(8,128)} %h_in.1, f32[8,32,128]{2,1,0:T(8,128)} %eps_in.1, f32[3,8,32,128]{3,2,1,0:T(8,128)} %ce_in.1, f32[3,8,32,128]{3,2,1,0:T(8,128)} %ch_in.1, s32[8,32,128]{2,1,0:T(8,128)} %ids_in.1), custom_call_target="tpu_custom_call" | custom-call | tf_op jit(solution)/shard_map/pallas_call | solution.py:322
  29.0 0.0 copy-start
  29.0 1.8 %copy.12 = f32[3,8,32,128]{3,2,1,0:T(8,128)} copy(f32[3,8,32,128]{3,2,1,0:T(8,128)} %get-tuple-element.12) | data formatting | bytes 786432
  30.8 0.0 copy-done
  30.9 0.0 copy-start.1
  30.9 0.7 %copy.13 = f32[3,8,32,128]{3,2,1,0:T(8,128)} copy(f32[3,8,32,128]{3,2,1,0:T(8,128)S(1)} %copy-done) | data formatting | bytes 786432
  31.6 0.0 copy-done.1
  31.6 0.5 %copy.14 = f32[64]{0:T(128)} copy(f32[64]{0:T(128)S(1)} %bitcast.1) | data formatting | bytes 512
Async XLA Ops:
  29.0 1.8 %copy-start = (f32[3,8,32,128]{3,2,1,0:T(8,128)S(1)}, f32[3,8,32,128]{3,2,1,0:T(8,128)}, u32[]{:S(2)}) copy-start(f32[3,8,32,128]{3,2,1,0:T(8,128)} %get-tuple-element.13) | copy-start | bytes 1179652
  30.9 0.8 %copy-start.1 = (f32[1,64]{1,0:T(1,128)S(1)}, f32[1,64]{1,0:T(1,128)}, u32[]{:S(2)}) copy-start(f32[1,64]{1,0:T(1,128)} %get-tuple-element.8) | copy-start | bytes 772

commit v5 on v4

--- a/solution.py
+++ b/solution.py
@@ -287,12 +287,17 @@
         for d in range(n):
             S[d] = both[d:d + 1, :]
 
-        @pl.loop(1, n)
-        def _(j):
-            to = (me + j) % n
-            pltpu.make_async_remote_copy(
-                S.at[to], R.at[me], as_sem, ar_sem,
-                device_id=(to // nb, to % nb), device_id_type=MESH).start()
+        for dg in range(ng):
+            to_grp = (grp + dg) % ng
+
+            def send_row(db, carry, to_grp=to_grp):
+                to_blk = (blk + db) % nb
+                pltpu.make_async_remote_copy(
+                    S.at[to_grp * nb + to_blk], R.at[me], as_sem, ar_sem,
+                    device_id=(to_grp, to_blk), device_id_type=MESH).start()
+                return carry
+
+            lax.fori_loop(0 if dg else 1, nb, send_row, 0, unroll=True)
 
         R[me] = S[me]
         rest = pl.ds(0, n - 1)

time: 32.3 us -> 32 us (level)
  no operation moved by 1% of the time
where the time goes in v5:
time: 32 us; the launch traced here: 31.8 us
  Pallas kernels  28.1 us (88%)
  local copies, waits for them, and re-layouts  3.08 us (10%)
  between operations  0.65 us (2%)
    pallas_call x1, Pallas kernels, local(): pl.pallas_call(make_kernel(ng, nb, nx, nz, ny), out_shape=(jax.ShapeDtype...  28.1 us
    unnamed x7, local copies, waits for them, and re-layouts  3.08 us

profile of v5, /device:TPU:0, one launch (start us, length us, event | category | flops | bytes accessed | tf_op | source)
XLA Modules:
  0.0 31.8 jit_solution(16231559093209734151)
XLA Ops:
  0.6 28.1 %shard_map.85 = (f32[3,8,32,128]{3,2,1,0:T(8,128)}, f32[3,8,32,128]{3,2,1,0:T(8,128)}, f32[1,64]{1,0:T(1,128)}) custom-call(f32[3,8,32,128]{3,2,1,0:T(8,128)} %e_in.1, f32[3,8,32,128]{3,2,1,0:T(8,128)} %h_in.1, f32[8,32,128]{2,1,0:T(8,128)} %eps_in.1, f32[3,8,32,128]{3,2,1,0:T(8,128)} %ce_in.1, f32[3,8,32,128]{3,2,1,0:T(8,128)} %ch_in.1, s32[8,32,128]{2,1,0:T(8,128)} %ids_in.1), custom_call_target="tpu_custom_call" | custom-call | tf_op jit(solution)/shard_map/pallas_call | solution.py:327
  28.7 0.0 copy-start
  28.7 1.8 %copy.12 = f32[3,8,32,128]{3,2,1,0:T(8,128)} copy(f32[3,8,32,128]{3,2,1,0:T(8,128)} %get-tuple-element.12) | data formatting | bytes 786432
  30.5 0.0 copy-done
  30.5 0.0 copy-start.1
  30.5 0.7 %copy.13 = f32[3,8,32,128]{3,2,1,0:T(8,128)} copy(f32[3,8,32,128]{3,2,1,0:T(8,128)S(1)} %copy-done) | data formatting | bytes 786432
  31.3 0.0 copy-done.1
  31.3 0.5 %copy.14 = f32[64]{0:T(128)} copy(f32[64]{0:T(128)S(1)} %bitcast.1) | data formatting | bytes 512
Async XLA Ops:
  28.7 1.8 %copy-start = (f32[3,8,32,128]{3,2,1,0:T(8,128)S(1)}, f32[3,8,32,128]{3,2,1,0:T(8,128)}, u32[]{:S(2)}) copy-start(f32[3,8,32,128]{3,2,1,0:T(8,128)} %get-tuple-element.13) | copy-start | bytes 1179652
  30.5 0.8 %copy-start.1 = (f32[1,64]{1,0:T(1,128)S(1)}, f32[1,64]{1,0:T(1,128)}, u32[]{:S(2)}) copy-start(f32[1,64]{1,0:T(1,128)} %get-tuple-element.8) | copy-start | bytes 772
